TPU v7x, 32 devices: a whole 2x2x4 slice. The times are simulated.
32 devices in a mesh: dp: 2 (over core), ctx: 16 (over z, y, x).
Axes of the slice: x: 2, y: 2, z: 4, core: 2. Of those that a mesh axis runs over, the one named last changes fastest.
Arguments:
- features: bfloat16 [2, 4096, 6144], P('dp', 'ctx'), may hold values from -6 to 6
- short_w: float32 [3, 6144], replicated, may hold values from -3.5 to 3.5
- long_h: float32 [128, 128], replicated, may hold values from -0.5 to 0.5
- skip_bias: float32 [2048], replicated, may hold values from -1 to 1
- cotangent: bfloat16 [2, 4096, 2048], P('dp', 'ctx'), may hold values from -6 to 6
Outputs:
- output: bfloat16 [2, 4096, 2048], P('dp', 'ctx')
- grad_features: bfloat16 [2, 4096, 6144], P('dp', 'ctx')
- grad_short: float32 [3, 6144], replicated
- grad_long: float32 [128, 128], replicated
- grad_skip: float32 [2048], replicated
All inputs are finite; a program needn't handle non-finite values.
Results may differ from a plain program's by a relative error of at most 0.008.
Values may be sent and summed in bfloat16 or wider, within the bound.
A program may use at most 128 MiB of HBM per device.

v0:
```python
import functools

import jax
import jax.numpy as jnp
from jax import lax
from jax.experimental import pallas as pl
from jax.experimental.pallas import tpu as pltpu
from jax.sharding import PartitionSpec as P

LANES = 128


def delayed(tile, edge, by):
    row = lax.broadcasted_iota(jnp.int32, tile.shape, 0)
    moved = pltpu.roll(tile, by, 0)
    if by == 1:
        return jnp.where(row == 0, edge[1:2], moved)
    return jnp.where(row == 0, edge[0:1], jnp.where(row == 1, edge[1:2], moved))


def advanced(tile, by):
    rows = tile.shape[0]
    row = lax.broadcasted_iota(jnp.int32, tile.shape, 0)
    return jnp.where(row < rows - by, pltpu.roll(tile, rows - by, 0), 0.0)


def filtered(feat_ref, w_ref, cols, edge, first, count):
    w = w_ref[:, cols]
    tile = feat_ref[first : first + count, cols].astype(jnp.float32)
    return w[0:1] * tile + w[1:2] * delayed(tile, edge, 1) + w[2:3] * delayed(tile, edge, 2)


def column_tile(stream, i, channels):
    return pl.ds(pl.multiple_of(stream * channels + i * LANES, LANES), LANES)


def halo_kernel(
    span, feat_ref, last_ref, cot_ref, w_ref, zt, gt, edge_ref,
    z_send, g_send, z_rim, g_rim, edge_got, sems,
):
    rows = feat_ref.shape[0]
    parts = z_send.shape[0]
    channels = parts * LANES
    blocks = rows // LANES
    f32, bf16 = jnp.float32, jnp.bfloat16
    length = span[1]
    dp, ctx = lax.axis_index("dp"), lax.axis_index("ctx")
    after, before = (dp, (ctx + 1) % length), (dp, (ctx + length - 1) % length)
    has_before = jnp.where(ctx > 0, 1.0, 0.0).astype(f32)
    has_after = jnp.where(ctx + 1 < length, 1.0, 0.0).astype(f32)

    def send(source, target, index, device):
        copy = pltpu.make_async_remote_copy(
            src_ref=source, dst_ref=target, send_sem=sems.at[index], recv_sem=sems.at[index + 1],
            device_id=device, device_id_type=pl.DeviceIdType.MESH,
        )
        copy.start()
        return copy

    barrier = pltpu.get_barrier_semaphore()
    for peer in (after, before):
        pl.semaphore_signal(barrier, inc=1, device_id=peer, device_id_type=pl.DeviceIdType.MESH)
    pl.semaphore_wait(barrier, 2)
    edge_copy = send(last_ref, edge_got, 0, after)

    def z_tail(i, _):
        pair = []
        for stream in (1, 2):
            cols = column_tile(stream, i, channels)
            edge = feat_ref[rows - LANES - 8 : rows - LANES, cols].astype(f32)[6:8]
            pair.append(filtered(feat_ref, w_ref, cols, edge, rows - LANES, LANES))
        z_send[i] = (pair[0] * pair[1]).astype(bf16)
        return 0

    lax.fori_loop(0, parts, z_tail, 0)
    z_copy = send(z_send, z_rim, 2, after)
    edge_copy.wait()
    edge_ref[...] = edge_got[...].astype(f32) * has_before

    def g_head(i, _):
        own = column_tile(0, i, channels)
        queries = filtered(feat_ref, w_ref, own, edge_ref[:, own], 0, LANES)
        g_send[i] = (cot_ref[:LANES, own].astype(f32) * queries).astype(bf16)
        return 0

    lax.fori_loop(0, parts, g_head, 0)
    g_copy = send(g_send, g_rim, 4, before)

    def featurize(i, _):
        own = column_tile(0, i, channels)
        made = []
        for stream in range(3):
            cols = column_tile(stream, i, channels)
            made.append(filtered(feat_ref, w_ref, cols, edge_ref[:, cols], 0, rows))
        z = (made[1] * made[2]).astype(bf16).astype(f32)
        g = (cot_ref[:, own].astype(f32) * made[0]).astype(bf16).astype(f32)
        for n in range(blocks):
            zt[n + 1, own] = z[n * LANES : (n + 1) * LANES].T
            gt[n, own] = g[n * LANES : (n + 1) * LANES].T
        return 0

    lax.fori_loop(0, parts, featurize, 0)
    z_copy.wait()
    g_copy.wait()

    def turn_rims(i, _):
        own = column_tile(0, i, channels)
        zt[0, own] = (z_rim[i].astype(f32) * has_before).T
        gt[blocks, own] = (g_rim[i].astype(f32) * has_after).T
        return 0

    lax.fori_loop(0, parts, turn_rims, 0)


def exchange(feat, cot, short_w):
    rows, wide = feat.shape
    channels = wide // 3
    parts = channels // LANES
    blocks = rows // LANES
    f32, bf16 = jnp.float32, jnp.bfloat16
    span = (lax.axis_size("dp"), lax.axis_size("ctx"))
    vmem = pl.BlockSpec(memory_space=pltpu.VMEM)
    rim = pltpu.VMEM((parts, LANES, LANES), bf16)
    turned = jax.ShapeDtypeStruct((blocks + 1, channels, LANES), f32)
    return pl.pallas_call(
        functools.partial(halo_kernel, span),
        out_shape=(turned, turned, jax.ShapeDtypeStruct((2, wide), f32)),
        in_specs=[vmem] * 4,
        out_specs=(vmem,) * 3,
        scratch_shapes=[
            rim, rim, rim, rim, pltpu.VMEM((2, wide), bf16), pltpu.SemaphoreType.DMA((6,)),
        ],
        compiler_params=pltpu.CompilerParams(collective_id=1, has_side_effects=True),
    )(feat, feat[rows - 2 :], cot, short_w)


def local_kernel(
    feat_ref, edge_ref, cot_ref, zt, gt, w_ref, h_ref, skip_ref,
    out_ref, gin_ref, head_ref, tail_ref, sums_ref,
    mt, gzt, lags,
):
    rows, channels = cot_ref.shape
    parts = channels // LANES
    groups = h_ref.shape[0]
    blocks = rows // LANES
    f32, bf16 = jnp.float32, jnp.bfloat16

    s_index = lax.broadcasted_iota(jnp.int32, (LANES, LANES), 0)
    t_index = lax.broadcasted_iota(jnp.int32, (LANES, LANES), 1)
    causal = t_index >= s_index

    def convolve(g, _):
        picked = pl.ds(g, parts, stride=LANES)
        zs = [zt[n, picked].astype(bf16) for n in range(blocks + 1)]
        gs = [gt[n, picked].astype(bf16) for n in range(blocks + 1)]
        z_win = jnp.concatenate(
            [jnp.concatenate([zs[n], zs[n + 1]], axis=1) for n in range(blocks)], axis=0
        )
        g_win = jnp.concatenate(
            [jnp.concatenate([gs[n], gs[n + 1]], axis=1) for n in range(blocks)], axis=0
        )
        g_own = jnp.concatenate(gs[:blocks], axis=0)
        taps = jnp.broadcast_to(h_ref[pl.ds(g, 1), :].astype(bf16).astype(f32), (LANES, LANES))
        circ = pltpu.roll(taps, 0, 1, stride=1, stride_axis=0)
        t0 = jnp.where(causal, circ, 0.0).astype(bf16)
        t1 = jnp.where(causal, 0.0, circ).astype(bf16)
        mixed = jnp.dot(z_win, jnp.concatenate([t1, t0], axis=0), preferred_element_type=f32)
        back = lax.dot_general(
            g_win, jnp.concatenate([t0, t1], axis=1), (((1,), (1,)), ((), ())),
            preferred_element_type=f32,
        )
        for n in range(blocks):
            mt[n, picked] = mixed[n * parts : (n + 1) * parts]
            gzt[n, picked] = back[n * parts : (n + 1) * parts]
        prod = lax.dot_general(z_win, g_own, (((0,), (0,)), ((), ())), preferred_element_type=f32)
        kept = jnp.where(causal, prod[LANES:], prod[:LANES])
        total = kept[:8]
        for low in range(8, LANES, 8):
            total = total + pltpu.roll(kept[low : low + 8], LANES - low, 1)
        lags[pl.ds(g, 8, stride=groups)] = total
        return 0

    lax.fori_loop(0, groups, convolve, 0, unroll=2)
    total = lags[:groups]
    for low in range(1, 8):
        total = total + pltpu.roll(lags[low * groups : (low + 1) * groups], LANES - low, 1)
    sums_ref[:groups] = total

    def finish(i, _):
        own = column_tile(0, i, channels)
        made = []
        for stream in range(3):
            cols = column_tile(stream, i, channels)
            made.append(filtered(feat_ref, w_ref, cols, edge_ref[:, cols], 0, rows))
        q, k, v = made
        z = (k * v).astype(bf16).astype(f32)
        g = (cot_ref[:, own].astype(f32) * q).astype(bf16).astype(f32)
        sums_ref[pl.ds(groups + i, 1), :] = jnp.sum(z * g, axis=0, keepdims=True)
        skip = skip_ref[:, own]
        mixed = jnp.concatenate([mt[n, own].T for n in range(blocks)], axis=0) + skip * z
        grad_z = jnp.concatenate([gzt[n, own].T for n in range(blocks)], axis=0) + skip * g
        out_ref[:, own] = (q * mixed).astype(bf16)
        grads = [cot_ref[:, own].astype(f32) * mixed, grad_z * v, grad_z * k]
        for stream in range(3):
            cols = column_tile(stream, i, channels)
            grad = grads[stream].astype(bf16).astype(f32)
            tile = feat_ref[:, cols].astype(f32)
            edge = edge_ref[:, cols]
            w = w_ref[:, cols]
            total = w[0:1] * grad + w[1:2] * advanced(grad, 1) + w[2:3] * advanced(grad, 2)
            gin_ref[:, cols] = total.astype(bf16)
            tail_ref[:, cols] = total[rows - 8 :]
            head_ref[:, cols] = grad[:2]
            for tap in range(3):
                past = delayed(tile, edge, tap) if tap else tile
                slot = groups + parts + (tap * 3 + stream) * parts + i
                sums_ref[pl.ds(slot, 1), :] = jnp.sum(grad * past, axis=0, keepdims=True)
        return 0

    lax.fori_loop(0, parts, finish, 0)
    used = groups + 10 * parts
    if used < sums_ref.shape[0]:
        sums_ref[used:] = jnp.zeros((sums_ref.shape[0] - used, LANES), f32)


def local_work(feat, edge, cot, zt, gt, short_w, filters, skip, sums):
    rows, wide = feat.shape
    channels = wide // 3
    blocks = rows // LANES
    f32, bf16 = jnp.float32, jnp.bfloat16
    vmem = pl.BlockSpec(memory_space=pltpu.VMEM)
    return pl.pallas_call(
        local_kernel,
        out_shape=(
            jax.ShapeDtypeStruct((rows, channels), bf16),
            jax.ShapeDtypeStruct((rows, wide), bf16),
            jax.ShapeDtypeStruct((2, wide), f32),
            jax.ShapeDtypeStruct((8, wide), f32),
            jax.ShapeDtypeStruct((sums, LANES), f32),
        ),
        in_specs=[vmem] * 8,
        out_specs=(vmem,) * 5,
        scratch_shapes=[
            pltpu.VMEM((blocks, channels, LANES), f32),
            pltpu.VMEM((blocks, channels, LANES), f32),
            pltpu.VMEM((8 * filters.shape[0], LANES), f32),
        ],
    )(feat, edge, cot, zt, gt, short_w, filters, skip)


INNER = 4


def sum_kernel(
    share, scale, span, sums_ref, head_ref, out_ref, ahead_ref,
    got_near, got_far, part, full, ahead,
    near_send, near_recv, far_send, far_recv, far_send2, far_recv2, near_send2, near_recv2, edge_sems,
):
    dp, ctx = lax.axis_index("dp"), lax.axis_index("ctx")
    dps, length = span
    near, far = dps * INNER, length // INNER
    outer, inner = ctx // INNER, ctx % INNER
    mine = dp * INNER + inner
    wide = far * share

    def near_peer(step):
        other = (mine + step) % near
        return other, (other // INNER, outer * INNER + other % INNER)

    def far_peer(step):
        other = (outer + step) % far
        return other, (dp, other * INNER + inner)

    def send(source, target, sems, device):
        copy = pltpu.make_async_remote_copy(
            src_ref=source, dst_ref=target, send_sem=sems[0], recv_sem=sems[1],
            device_id=device, device_id_type=pl.DeviceIdType.MESH,
        )
        copy.start()
        return copy

    after, before = (dp, (ctx + 1) % length), (dp, (ctx + length - 1) % length)
    peers = [near_peer(step)[1] for step in range(1, near)]
    peers += [far_peer(step)[1] for step in range(1, far)] + [after, before]
    barrier = pltpu.get_barrier_semaphore()
    for peer in peers:
        pl.semaphore_signal(barrier, inc=1, device_id=peer, device_id_type=pl.DeviceIdType.MESH)
    pl.semaphore_wait(barrier, len(peers))

    copies = []
    for step in range(1, near):
        other, device = near_peer(step)
        copies.append(send(
            sums_ref.at[pl.ds(other * wide, wide)], got_near.at[step - 1],
            (near_send.at[step - 1], near_recv.at[step - 1]), device,
        ))
    edge_copy = send(head_ref, ahead, (edge_sems.at[0], edge_sems.at[1]), before)
    total = sums_ref[pl.ds(mine * wide, wide)]
    for step, copy in enumerate(copies):
        copy.wait()
        total = total + got_near[step]
    part[...] = total

    copies = []
    for step in range(1, far):
        other, device = far_peer(step)
        copies.append(send(
            part.at[pl.ds(other * share, share)], got_far.at[step - 1],
            (far_send.at[step - 1], far_recv.at[step - 1]), device,
        ))
    total = part[pl.ds(outer * share, share)]
    for step, copy in enumerate(copies):
        copy.wait()
        total = total + got_far[step]
    place = pl.ds(mine * wide + outer * share, share)
    full[place] = total * scale

    copies = [
        send(
            full.at[place], full.at[place],
            (far_send2.at[step - 1], far_recv2.at[step - 1]), far_peer(step)[1],
        )
        for step in range(1, far)
    ]
    for copy in copies:
        copy.wait()
    place = pl.ds(mine * wide, wide)
    copies = [
        send(
            full.at[place], full.at[place],
            (near_send2.at[step - 1], near_recv2.at[step - 1]), near_peer(step)[1],
        )
        for step in range(1, near)
    ]
    for copy in copies:
        copy.wait()
    edge_copy.wait()
    out_ref[...] = full[...]
    ahead_ref[...] = ahead[...]


def total_over_devices(sums, head, share, scale):
    f32 = jnp.float32
    span = (lax.axis_size("dp"), lax.axis_size("ctx"))
    near, far = span[0] * INNER, span[1] // INNER
    rows = sums.shape[0]
    vmem = pl.BlockSpec(memory_space=pltpu.VMEM)
    dma = pltpu.SemaphoreType.DMA
    totals, ahead = pl.pallas_call(
        functools.partial(sum_kernel, share, scale, span),
        out_shape=(
            jax.ShapeDtypeStruct((rows, 1, LANES), f32),
            jax.ShapeDtypeStruct(head.shape, head.dtype),
        ),
        in_specs=[vmem] * 2,
        out_specs=(vmem,) * 2,
        scratch_shapes=[
            pltpu.VMEM((near - 1, far * share, 1, LANES), f32),
            pltpu.VMEM((max(far - 1, 1), share, 1, LANES), f32),
            pltpu.VMEM((far * share, 1, LANES), f32),
            pltpu.VMEM((rows, 1, LANES), f32),
            pltpu.VMEM(head.shape, head.dtype),
            dma((near - 1,)), dma((near - 1,)),
            dma((max(far - 1, 1),)), dma((max(far - 1, 1),)),
            dma((max(far - 1, 1),)), dma((max(far - 1, 1),)),
            dma((near - 1,)), dma((near - 1,)),
            dma((2,)),
        ],
        compiler_params=pltpu.CompilerParams(
            collective_id=0, has_side_effects=True, vmem_limit_bytes=16 * 1024 * 1024
        ),
    )(sums.reshape(rows, 1, LANES), head)
    return totals.reshape(rows, LANES), ahead


def body(features, short_w, long_h, skip_bias, cotangent):
    f32, bf16 = jnp.float32, jnp.bfloat16
    feat = features[0]
    cot = cotangent[0]
    rows = feat.shape[0]
    channels = skip_bias.shape[0]
    groups, taps = long_h.shape
    zt, gt, edge = exchange(feat, cot, short_w)
    devices = lax.axis_size("dp") * lax.axis_size("ctx")
    used = groups + 10 * (channels // LANES)
    share = -(-used // devices)
    output, grad_in, head, last, sums = local_work(
        feat, edge, cot, zt, gt, short_w, long_h, skip_bias[None], share * devices
    )
    scale = (devices * rows) ** (-0.5)
    totals, ahead = total_over_devices(sums, head, share, scale)
    ahead = jnp.where(lax.axis_index("ctx") + 1 < lax.axis_size("ctx"), ahead, 0.0)
    row0 = last[6] + short_w[2] * ahead[0]
    row1 = last[7] + short_w[1] * ahead[0] + short_w[2] * ahead[1]
    grad_in = lax.dynamic_update_slice(
        grad_in, jnp.stack([row0, row1]).astype(bf16), (rows - 2, 0)
    )
    parts = channels // LANES
    return (
        output[None],
        grad_in[None],
        totals[groups + parts : used].reshape(short_w.shape),
        totals[:groups],
        totals[groups : groups + parts].reshape(channels),
    )


def solution(mesh):
    return jax.shard_map(
        body,
        mesh=mesh,
        in_specs=(P("dp", "ctx", None), P(), P(), P(), P("dp", "ctx", None)),
        out_specs=(P("dp", "ctx", None), P("dp", "ctx", None), P(), P(), P()),
        check_vma=False,
    )
```

profile of v0, /device:TPU:0, one launch (start us, length us, event | category | flops | bytes accessed | tf_op | source)
XLA Modules:
  0.0 102.9 jit_solution(1321836976409884758)
XLA Ops:
  0.6 1.5 %slice_bitcast_fusion.last_ref = bf16[2,6144]{1,0:T(2,128)(2,1)} fusion(bf16[1,256,6144]{2,1,0:T(8,128)(2,1)} %param.5), kind=kLoop, calls=%fused_computation.7 | loop fusion | bytes 49152 | tf_op jit(solution)/shard_map/slice | solution.py:134
  2.2 37.0 %shard_map.92 = (f32[3,2048,128]{2,1,0:T(8,128)}, f32[3,2048,128]{2,1,0:T(8,128)}, f32[2,6144]{1,0:T(2,128)}) custom-call(bf16[256,6144]{1,0:T(8,128)(2,1)} %bitcast.15, bf16[2,6144]{1,0:T(2,128)(2,1)} %slice_bitcast_fusion.last_ref, bf16[256,2048]{1,0:T(8,128)(2,1)} %bitcast.17, f32[3,6144]{1,0:T(4,128)} %w_ref.3), custom_call_target="tpu_custom_call" | custom-call | tf_op jit(solution)/shard_map/pallas_call | solution.py:125
  39.2 0.0 copy-start.2
  39.2 39.7 %shard_map.93 = (bf16[256,2048]{1,0:T(8,128)(2,1)}, bf16[256,6144]{1,0:T(8,128)(2,1)}, f32[2,6144]{1,0:T(2,128)}, f32[8,6144]{1,0:T(8,128)}, f32[288,128]{1,0:T(8,128)}) custom-call(bf16[256,6144]{1,0:T(8,128)(2,1)} %bitcast.16, f32[2,6144]{1,0:T(2,128)} %get-tuple-element.15.edge_ref, bf16[256,2048]{1,0:T(8,128)(2,1)} %bitcast.18, ...), custom_call_target="tpu_custom_call" | custom-call | tf_op jit(solution)/shard_map/pallas_call | solution.py:232
  78.9 0.0 copy-start
  78.9 0.9 copy-done
  79.8 0.0 copy-start.1
  79.8 0.8 copy-done.1
  80.6 18.3 %shard_map.94 = (f32[288,1,128]{2,1,0:T(1,128)S(1)}, f32[2,6144]{1,0:T(2,128)S(1)}) custom-call(f32[288,1,128]{2,1,0:T(1,128)S(1)} %bitcast.14, f32[2,6144]{1,0:T(2,128)S(1)} %copy-done.1), custom_call_target="tpu_custom_call" | custom-call | tf_op jit(solution)/shard_map/pallas_call | solution.py:349
  98.9 0.0 copy-done.2
  98.9 1.1 %convert_bitcast_fusion.1 = (bf16[1,1,6144]{2,1,0:T(2,128)(2,1)S(1)}, bf16[1,1,6144]{2,1,0:T(2,128)(2,1)S(1)}) fusion(f32[8,6144]{1,0:T(8,128)} %get-tuple-element.20, f32[2,6144]{1,0:T(2,128)S(1)} %broadcast_select_fusion, f32[3,6144]{1,0:T(4,128)S(1)} %copy-done.2), kind=kLoop, calls=%fused_computation.6 | loop fusion | flops 49152 | bytes 172032 | tf_op jit(solution)/shard_map/stack | solution.py:396
  100.1 0.7 maximum_dynamic-update-slice_fusion
  100.8 0.2 slice_reduce_fusion
  101.0 0.7 reshape.60
  101.6 0.6 slice.49
  102.3 0.6 slice.51
  (1 shorter events, 0.0 us)
Async XLA Ops:
  39.2 59.8 %copy-start.2 = (f32[3,6144]{1,0:T(4,128)S(1)}, f32[3,6144]{1,0:T(4,128)}, u32[]{:S(2)}) copy-start(f32[3,6144]{1,0:T(4,128)} %w_ref.3) | copy-start | bytes 221188
  78.9 0.9 copy-start
  79.8 0.8 copy-start.1
where the time goes:
time: 103 us
  Pallas kernels  95 us (92%)
  local copies, waits for them, and re-layouts  5.34 us (5%)
  other arithmetic  1.84 us (2%)
    pallas_call x1, Pallas kernels, local_work(): pl.pallas_call(local_kernel, out_shape=(jax.ShapeDtypeStruct((rows, chann...  39.7 us
    pallas_call x1, Pallas kernels, exchange(): pl.pallas_call(functools.partial(halo_kernel, span), out_shape=(turned, t...  37 us
    pallas_call x1, Pallas kernels, total_over_devices(): pl.pallas_call(functools.partial(sum_kernel, share, scale, span), out_sha...  18.3 us

commit v1 on v0

--- a/solution.py
+++ b/solution.py
@@ -8,6 +8,7 @@
 from jax.sharding import PartitionSpec as P
 
 LANES = 128
+PITCH = 132
 
 
 def delayed(tile, edge, by):
@@ -28,6 +29,14 @@
     w = w_ref[:, cols]
     tile = feat_ref[first : first + count, cols].astype(jnp.float32)
     return w[0:1] * tile + w[1:2] * delayed(tile, edge, 1) + w[2:3] * delayed(tile, edge, 2)
+
+
+def turned_tile(i):
+    return pl.ds(i * PITCH, LANES)
+
+
+def turned_rows(channels):
+    return channels // LANES * PITCH
 
 
 def column_tile(stream, i, channels):
@@ -95,8 +104,8 @@
         z = (made[1] * made[2]).astype(bf16).astype(f32)
         g = (cot_ref[:, own].astype(f32) * made[0]).astype(bf16).astype(f32)
         for n in range(blocks):
-            zt[n + 1, own] = z[n * LANES : (n + 1) * LANES].T
-            gt[n, own] = g[n * LANES : (n + 1) * LANES].T
+            zt[n + 1, turned_tile(i)] = z[n * LANES : (n + 1) * LANES].T
+            gt[n, turned_tile(i)] = g[n * LANES : (n + 1) * LANES].T
         return 0
 
     lax.fori_loop(0, parts, featurize, 0)
@@ -104,7 +113,7 @@
     g_copy.wait()
 
     def turn_rims(i, _):
-        own = column_tile(0, i, channels)
+        own = turned_tile(i)
         zt[0, own] = (z_rim[i].astype(f32) * has_before).T
         gt[blocks, own] = (g_rim[i].astype(f32) * has_after).T
         return 0
@@ -121,7 +130,7 @@
     span = (lax.axis_size("dp"), lax.axis_size("ctx"))
     vmem = pl.BlockSpec(memory_space=pltpu.VMEM)
     rim = pltpu.VMEM((parts, LANES, LANES), bf16)
-    turned = jax.ShapeDtypeStruct((blocks + 1, channels, LANES), f32)
+    turned = jax.ShapeDtypeStruct((blocks + 1, turned_rows(channels), LANES), f32)
     return pl.pallas_call(
         functools.partial(halo_kernel, span),
         out_shape=(turned, turned, jax.ShapeDtypeStruct((2, wide), f32)),
@@ -150,7 +159,7 @@
     causal = t_index >= s_index
 
     def convolve(g, _):
-        picked = pl.ds(g, parts, stride=LANES)
+        picked = pl.ds(g, parts, stride=PITCH)
         zs = [zt[n, picked].astype(bf16) for n in range(blocks + 1)]
         gs = [gt[n, picked].astype(bf16) for n in range(blocks + 1)]
         z_win = jnp.concatenate(
@@ -180,7 +189,7 @@
         lags[pl.ds(g, 8, stride=groups)] = total
         return 0
 
-    lax.fori_loop(0, groups, convolve, 0, unroll=2)
+    lax.fori_loop(0, groups, convolve, 0, unroll=8)
     total = lags[:groups]
     for low in range(1, 8):
         total = total + pltpu.roll(lags[low * groups : (low + 1) * groups], LANES - low, 1)
@@ -197,8 +206,8 @@
         g = (cot_ref[:, own].astype(f32) * q).astype(bf16).astype(f32)
         sums_ref[pl.ds(groups + i, 1), :] = jnp.sum(z * g, axis=0, keepdims=True)
         skip = skip_ref[:, own]
-        mixed = jnp.concatenate([mt[n, own].T for n in range(blocks)], axis=0) + skip * z
-        grad_z = jnp.concatenate([gzt[n, own].T for n in range(blocks)], axis=0) + skip * g
+        mixed = jnp.concatenate([mt[n, turned_tile(i)].T for n in range(blocks)], axis=0) + skip * z
+        grad_z = jnp.concatenate([gzt[n, turned_tile(i)].T for n in range(blocks)], axis=0) + skip * g
         out_ref[:, own] = (q * mixed).astype(bf16)
         grads = [cot_ref[:, own].astype(f32) * mixed, grad_z * v, grad_z * k]
         for stream in range(3):
@@ -241,8 +250,8 @@
         in_specs=[vmem] * 8,
         out_specs=(vmem,) * 5,
         scratch_shapes=[
-            pltpu.VMEM((blocks, channels, LANES), f32),
-            pltpu.VMEM((blocks, channels, LANES), f32),
+            pltpu.VMEM((blocks, turned_rows(channels), LANES), f32),
+            pltpu.VMEM((blocks, turned_rows(channels), LANES), f32),
             pltpu.VMEM((8 * filters.shape[0], LANES), f32),
         ],
     )(feat, edge, cot, zt, gt, short_w, filters, skip)

time: 103 us -> 88.5 us (0.86)
  Pallas kernels: 95 us -> 80.4 us
    pallas_call x1, Pallas kernels: 39.7 us -> 25 us  [local_work(): pl.pallas_call(local_kernel, out_shape=(jax.ShapeDtypeStruct((rows, chann...]
where the time goes in v1:
time: 88.5 us; the launch traced here: 88.2 us
  Pallas kernels  80.4 us (91%)
  local copies, waits for them, and re-layouts  5.34 us (6%)
  other arithmetic  1.84 us (2%)
    pallas_call x1, Pallas kernels, exchange(): pl.pallas_call(functools.partial(halo_kernel, span), out_shape=(turned, t...  37 us
    pallas_call x1, Pallas kernels, local_work(): pl.pallas_call(local_kernel, out_shape=(jax.ShapeDtypeStruct((rows, chann...  25 us
    pallas_call x1, Pallas kernels, total_over_devices(): pl.pallas_call(functools.partial(sum_kernel, share, scale, span), out_sha...  18.3 us

profile of v1, /device:TPU:0, one launch (start us, length us, event | category | flops | bytes accessed | tf_op | source)
XLA Modules:
  0.0 88.2 jit_solution(8466663921589883565)
XLA Ops:
  0.6 1.5 %slice_bitcast_fusion.last_ref = bf16[2,6144]{1,0:T(2,128)(2,1)} fusion(bf16[1,256,6144]{2,1,0:T(8,128)(2,1)} %param.5), kind=kLoop, calls=%fused_computation.7 | loop fusion | bytes 49152 | tf_op jit(solution)/shard_map/slice | solution.py:143
  2.2 37.0 %shard_map.92 = (f32[3,2112,128]{2,1,0:T(8,128)}, f32[3,2112,128]{2,1,0:T(8,128)}, f32[2,6144]{1,0:T(2,128)}) custom-call(bf16[256,6144]{1,0:T(8,128)(2,1)} %bitcast.15, bf16[2,6144]{1,0:T(2,128)(2,1)} %slice_bitcast_fusion.last_ref, bf16[256,2048]{1,0:T(8,128)(2,1)} %bitcast.17, f32[3,6144]{1,0:T(4,128)} %w_ref.3), custom_call_target="tpu_custom_call" | custom-call | tf_op jit(solution)/shard_map/pallas_call | solution.py:134
  39.2 0.0 copy-start.2
  39.2 25.0 %shard_map.93 = (bf16[256,2048]{1,0:T(8,128)(2,1)}, bf16[256,6144]{1,0:T(8,128)(2,1)}, f32[2,6144]{1,0:T(2,128)}, f32[8,6144]{1,0:T(8,128)}, f32[288,128]{1,0:T(8,128)}) custom-call(bf16[256,6144]{1,0:T(8,128)(2,1)} %bitcast.16, f32[2,6144]{1,0:T(2,128)} %get-tuple-element.15.edge_ref, bf16[256,2048]{1,0:T(8,128)(2,1)} %bitcast.18, ...), custom_call_target="tpu_custom_call" | custom-call | tf_op jit(solution)/shard_map/pallas_call | solution.py:241
  64.2 0.0 copy-start
  64.2 0.9 %copy-done = f32[288,128]{1,0:T(8,128)S(1)} copy-done((f32[288,128]{1,0:T(8,128)S(1)}, f32[288,128]{1,0:T(8,128)}, u32[]{:S(2)}) %copy-start) | copy-done | bytes 147480
  65.1 0.0 copy-start.1
  65.1 0.8 copy-done.1
  65.9 18.3 %shard_map.94 = (f32[288,1,128]{2,1,0:T(1,128)S(1)}, f32[2,6144]{1,0:T(2,128)S(1)}) custom-call(f32[288,1,128]{2,1,0:T(1,128)S(1)} %bitcast.14, f32[2,6144]{1,0:T(2,128)S(1)} %copy-done.1), custom_call_target="tpu_custom_call" | custom-call | tf_op jit(solution)/shard_map/pallas_call | solution.py:358
  84.3 0.0 copy-done.2
  84.3 1.1 %convert_bitcast_fusion.1 = (bf16[1,1,6144]{2,1,0:T(2,128)(2,1)S(1)}, bf16[1,1,6144]{2,1,0:T(2,128)(2,1)S(1)}) fusion(f32[8,6144]{1,0:T(8,128)} %get-tuple-element.20, f32[2,6144]{1,0:T(2,128)S(1)} %broadcast_select_fusion, f32[3,6144]{1,0:T(4,128)S(1)} %copy-done.2), kind=kLoop, calls=%fused_computation.6 | loop fusion | flops 49152 | bytes 172032 | tf_op jit(solution)/shard_map/stack | solution.py:405
  85.5 0.7 maximum_dynamic-update-slice_fusion
  86.1 0.2 slice_reduce_fusion
  86.3 0.7 reshape.60
  87.0 0.6 slice.49
  87.6 0.6 slice.51
  (1 shorter events, 0.0 us)
Async XLA Ops:
  39.2 45.1 %copy-start.2 = (f32[3,6144]{1,0:T(4,128)S(1)}, f32[3,6144]{1,0:T(4,128)}, u32[]{:S(2)}) copy-start(f32[3,6144]{1,0:T(4,128)} %w_ref.3) | copy-start | bytes 221188
  64.2 0.9 %copy-start = (f32[288,128]{1,0:T(8,128)S(1)}, f32[288,128]{1,0:T(8,128)}, u32[]{:S(2)}) copy-start(f32[288,128]{1,0:T(8,128)} %get-tuple-element.21) | copy-start | bytes 442372
  65.1 0.8 copy-start.1

commit v2 on v1

v2 whole, which is shorter than its diff:
```python
import functools

import jax
import jax.numpy as jnp
from jax import lax
from jax.experimental import pallas as pl
from jax.experimental.pallas import tpu as pltpu
from jax.sharding import PartitionSpec as P

LANES = 128
PITCH = 132


def delayed(tile, edge, by):
    row = lax.broadcasted_iota(jnp.int32, tile.shape, 0)
    moved = pltpu.roll(tile, by, 0)
    if by == 1:
        return jnp.where(row == 0, edge[1:2], moved)
    return jnp.where(row == 0, edge[0:1], jnp.where(row == 1, edge[1:2], moved))


def filtered(feat_ref, w_ref, cols, edge, first, count):
    w = w_ref[:, cols]
    tile = feat_ref[first : first + count, cols].astype(jnp.float32)
    return w[0:1] * tile + w[1:2] * delayed(tile, edge, 1) + w[2:3] * delayed(tile, edge, 2)


def turned_tile(i):
    return pl.ds(i * PITCH, LANES)


def turned_rows(channels):
    return channels // LANES * PITCH


def column_tile(stream, i, channels):
    return pl.ds(pl.multiple_of(stream * channels + i * LANES, LANES), LANES)


def diagonals(kept):
    total = kept[:8]
    for low in range(8, LANES, 8):
        total = total + pltpu.roll(kept[low : low + 8], LANES - low, 1)
    return total


def main_kernel(
    span, feat_hbm, cot_hbm, w_ref, h_ref, skip_ref,
    out_ref, gin_ref, head_ref, tail_ref, sums_ref,
    feat_ref, cot_ref, staged, made, grads, zt, gt, rims, mt, gzt, t1_all, lags,
    z_send, g_send, z_rim, g_rim, edge_send, edge_got, edge_ref, sems, load_sems,
):
    rows, channels = cot_ref.shape
    parts = channels // LANES
    groups = h_ref.shape[0]
    blocks = rows // LANES
    f32, bf16 = jnp.float32, jnp.bfloat16
    length = span[1]
    dp, ctx = lax.axis_index("dp"), lax.axis_index("ctx")
    after, before = (dp, (ctx + 1) % length), (dp, (ctx + length - 1) % length)
    has_before = jnp.where(ctx > 0, 1.0, 0.0).astype(f32)
    has_after = jnp.where(ctx + 1 < length, 1.0, 0.0).astype(f32)

    early = rows - LANES - 16
    loads = []
    for source, target in (
        (feat_hbm.at[early:, channels:], feat_ref.at[early:, channels:]),
        (feat_hbm.at[:, :channels], feat_ref.at[:, :channels]),
        (cot_hbm, cot_ref),
        (feat_hbm.at[:early, channels:], feat_ref.at[:early, channels:]),
    ):
        copy = pltpu.make_async_copy(source, target, load_sems.at[len(loads)])
        copy.start()
        loads.append(copy)

    def send(source, target, index, device):
        copy = pltpu.make_async_remote_copy(
            src_ref=source, dst_ref=target, send_sem=sems.at[index], recv_sem=sems.at[index + 1],
            device_id=device, device_id_type=pl.DeviceIdType.MESH,
        )
        copy.start()
        return copy

    barrier = pltpu.get_barrier_semaphore()
    for peer in (after, before):
        pl.semaphore_signal(barrier, inc=1, device_id=peer, device_id_type=pl.DeviceIdType.MESH)

    loads[0].wait()
    loads[1].wait()
    edge_send[...] = feat_ref[rows - 16 :, :].astype(f32)[14:16].astype(bf16)
    pl.semaphore_wait(barrier, 2)
    edge_copy = send(edge_send, edge_got, 0, after)

    def z_tail(i, _):
        pair = []
        for stream in (1, 2):
            cols = column_tile(stream, i, channels)
            edge = feat_ref[early : early + 16, cols].astype(f32)[14:16]
            pair.append(filtered(feat_ref, w_ref, cols, edge, rows - LANES, LANES))
        z_send[i] = (pair[0] * pair[1]).astype(bf16)
        return 0

    half = parts // 2
    copies = []
    for n in range(2):
        piece = pl.ds(n * half, half)
        lax.fori_loop(n * half, (n + 1) * half, z_tail, 0)
        copies.append(send(z_send.at[piece], z_rim.at[piece], 2 + 2 * n, after))
    edge_copy.wait()
    edge_ref[...] = edge_got[...].astype(f32) * has_before
    loads[2].wait()

    def g_head(i, _):
        own = column_tile(0, i, channels)
        queries = filtered(feat_ref, w_ref, own, edge_ref[:, own], 0, LANES)
        g_send[i] = (cot_ref[:LANES, own].astype(f32) * queries).astype(bf16)
        return 0

    for n in range(2):
        piece = pl.ds(n * half, half)
        lax.fori_loop(n * half, (n + 1) * half, g_head, 0)
        copies.append(send(g_send.at[piece], g_rim.at[piece], 6 + 2 * n, before))
    loads[3].wait()

    def featurize(i, _):
        own = column_tile(0, i, channels)
        for stream in range(3):
            cols = column_tile(stream, i, channels)
            slot = stream * parts + i
            w = w_ref[:, cols]
            staged[slot, 6:8] = edge_ref[:, cols]
            staged[slot, 8:] = feat_ref[:, cols].astype(f32)
            made[slot] = (
                w[0:1] * staged[slot, 8 : 8 + rows]
                + w[1:2] * staged[slot, 7 : 7 + rows]
                + w[2:3] * staged[slot, 6 : 6 + rows]
            )
        total = jnp.zeros((1, LANES), f32)
        for n in range(blocks):
            at = pl.ds(n * LANES, LANES)
            z = (made[parts + i, at] * made[2 * parts + i, at]).astype(bf16).astype(f32)
            g = (cot_ref[at, own].astype(f32) * made[i, at]).astype(bf16).astype(f32)
            total = total + jnp.sum(z * g, axis=0, keepdims=True)
            zt[n, turned_tile(i)] = z.T
            gt[n, turned_tile(i)] = g.T
        sums_ref[pl.ds(groups + i, 1), :] = total
        return 0

    lax.fori_loop(0, parts, featurize, 0)

    s_index = lax.broadcasted_iota(jnp.int32, (LANES, LANES), 0)
    t_index = lax.broadcasted_iota(jnp.int32, (LANES, LANES), 1)
    causal = t_index >= s_index
    contract = lambda a, b, da, db: lax.dot_general(
        a, b, (((da,), (db,)), ((), ())), preferred_element_type=f32
    )

    def convolve(g, _):
        picked = pl.ds(g, parts, stride=PITCH)
        zs = [zt[n, picked].astype(bf16) for n in range(blocks)]
        gs = [gt[n, picked].astype(bf16) for n in range(blocks)]
        none = jnp.zeros((parts, LANES), bf16)
        z_win = jnp.concatenate(
            [jnp.concatenate([a, b], axis=1) for a, b in zip([none] + zs, zs)], axis=0
        )
        g_win = jnp.concatenate(
            [jnp.concatenate([a, b], axis=1) for a, b in zip(gs, gs[1:] + [none])], axis=0
        )
        taps = jnp.broadcast_to(h_ref[pl.ds(g, 1), :].astype(bf16).astype(f32), (LANES, LANES))
        circ = pltpu.roll(taps, 0, 1, stride=1, stride_axis=0)
        t0 = jnp.where(causal, circ, 0.0).astype(bf16)
        t1 = jnp.where(causal, 0.0, circ).astype(bf16)
        t1_all[pl.ds(pl.multiple_of(g * LANES, LANES), LANES)] = t1
        mixed = contract(z_win, jnp.concatenate([t1, t0], axis=0), 1, 0)
        back = contract(g_win, jnp.concatenate([t0, t1], axis=1), 1, 1)
        for n in range(blocks):
            mt[n, picked] = mixed[n * parts : (n + 1) * parts]
            gzt[n, picked] = back[n * parts : (n + 1) * parts]
        prod = contract(z_win, jnp.concatenate(gs, axis=0), 0, 0)
        kept = jnp.where(causal, prod[LANES:], prod[:LANES])
        lags[pl.ds(g, 8, stride=PITCH)] = diagonals(kept)
        return 0

    lax.fori_loop(0, groups, convolve, 0, unroll=8)
    for copy in copies:
        copy.wait()

    def turn_rims(i, _):
        rims[0, turned_tile(i)] = (z_rim[i].astype(f32) * has_before).T
        rims[1, turned_tile(i)] = (g_rim[i].astype(f32) * has_after).T
        return 0

    lax.fori_loop(0, parts, turn_rims, 0, unroll=2)

    def convolve_rims(g, _):
        picked = pl.ds(g, parts, stride=PITCH)
        zr = rims[0, picked].astype(bf16)
        gr = rims[1, picked].astype(bf16)
        t1 = t1_all[pl.ds(pl.multiple_of(g * LANES, LANES), LANES)]
        mt[0, picked] += contract(zr, t1, 1, 0)
        gzt[blocks - 1, picked] += contract(gr, t1, 1, 1)
        prod = contract(zr, gt[0, picked].astype(bf16), 0, 0)
        lags[pl.ds(g, 8, stride=PITCH)] += diagonals(jnp.where(causal, 0.0, prod))
        return 0

    lax.fori_loop(0, groups, convolve_rims, 0, unroll=8)
    total = lags[:groups]
    for low in range(1, 8):
        total = total + pltpu.roll(lags[low * PITCH : low * PITCH + groups], LANES - low, 1)
    sums_ref[:groups] = total
    grads[:, rows:] = jnp.zeros((3, 8, LANES), f32)

    def finish(i, _):
        own = column_tile(0, i, channels)
        skip = skip_ref[:, own]
        for n in range(blocks):
            at = pl.ds(n * LANES, LANES)
            q, k, v = made[i, at], made[parts + i, at], made[2 * parts + i, at]
            ct = cot_ref[at, own].astype(f32)
            z = (k * v).astype(bf16).astype(f32)
            g = (ct * q).astype(bf16).astype(f32)
            mixed = mt[n, turned_tile(i)].T + skip * z
            grad_z = gzt[n, turned_tile(i)].T + skip * g
            out_ref[at, own] = (q * mixed).astype(bf16)
            grads[0, at] = (ct * mixed).astype(bf16).astype(f32)
            grads[1, at] = (grad_z * v).astype(bf16).astype(f32)
            grads[2, at] = (grad_z * k).astype(bf16).astype(f32)
        for stream in range(3):
            cols = column_tile(stream, i, channels)
            slot = stream * parts + i
            w = w_ref[:, cols]
            totals = [jnp.zeros((1, LANES), f32) for _ in range(3)]
            for n in range(blocks):
                low = n * LANES
                grad = grads[stream, low : low + LANES]
                new = (
                    w[0:1] * grad
                    + w[1:2] * grads[stream, low + 1 : low + 1 + LANES]
                    + w[2:3] * grads[stream, low + 2 : low + 2 + LANES]
                )
                gin_ref[low : low + LANES, cols] = new.astype(bf16)
                for tap in range(3):
                    past = staged[slot, 8 - tap + low : 8 - tap + low + LANES]
                    totals[tap] = totals[tap] + jnp.sum(grad * past, axis=0, keepdims=True)
            tail_ref[:, cols] = new[LANES - 8 :]
            head_ref[:, cols] = grads[stream, 0:2]
            for tap in range(3):
                line = groups + parts + (tap * 3 + stream) * parts + i
                sums_ref[pl.ds(line, 1), :] = totals[tap]
        return 0

    lax.fori_loop(0, parts, finish, 0)
    used = groups + 10 * parts
    if used < sums_ref.shape[0]:
        sums_ref[used:] = jnp.zeros((sums_ref.shape[0] - used, LANES), f32)


def main_work(feat, cot, short_w, filters, skip, sums):
    rows, wide = feat.shape
    channels = wide // 3
    parts = channels // LANES
    blocks = rows // LANES
    groups = filters.shape[0]
    f32, bf16 = jnp.float32, jnp.bfloat16
    span = (lax.axis_size("dp"), lax.axis_size("ctx"))
    vmem = pl.BlockSpec(memory_space=pltpu.VMEM)
    hbm = pl.BlockSpec(memory_space=pl.ANY)
    rim = pltpu.VMEM((parts, LANES, LANES), bf16)
    turned = pltpu.VMEM((blocks, turned_rows(channels), LANES), f32)
    return pl.pallas_call(
        functools.partial(main_kernel, span),
        out_shape=(
            jax.ShapeDtypeStruct((rows, channels), bf16),
            jax.ShapeDtypeStruct((rows, wide), bf16),
            jax.ShapeDtypeStruct((2, wide), f32),
            jax.ShapeDtypeStruct((8, wide), f32),
            jax.ShapeDtypeStruct((sums, LANES), f32),
        ),
        in_specs=[hbm, hbm, vmem, vmem, vmem],
        out_specs=(vmem,) * 5,
        scratch_shapes=[
            pltpu.VMEM((rows, wide), bf16),
            pltpu.VMEM((rows, channels), bf16),
            pltpu.VMEM((3 * parts, rows + 8, LANES), f32),
            pltpu.VMEM((3 * parts, rows, LANES), f32),
            pltpu.VMEM((3, rows + 8, LANES), f32),
            turned, turned,
            pltpu.VMEM((2, turned_rows(channels), LANES), f32),
            turned, turned,
            pltpu.VMEM((groups * LANES, LANES), bf16),
            pltpu.VMEM((8 * PITCH, LANES), f32),
            rim, rim, rim, rim,
            pltpu.VMEM((2, wide), bf16), pltpu.VMEM((2, wide), bf16), pltpu.VMEM((2, wide), f32),
            pltpu.SemaphoreType.DMA((10,)), pltpu.SemaphoreType.DMA((4,)),
        ],
        compiler_params=pltpu.CompilerParams(
            collective_id=1, has_side_effects=True, vmem_limit_bytes=60 * 1024 * 1024
        ),
    )(feat, cot, short_w, filters, skip)


INNER = 4


def sum_kernel(
    share, scale, span, sums_ref, head_ref, out_ref, ahead_ref,
    got_near, got_far, part, full, ahead,
    near_send, near_recv, far_send, far_recv, far_send2, far_recv2, near_send2, near_recv2, edge_sems,
):
    dp, ctx = lax.axis_index("dp"), lax.axis_index("ctx")
    dps, length = span
    near, far = dps * INNER, length // INNER
    outer, inner = ctx // INNER, ctx % INNER
    mine = dp * INNER + inner
    wide = far * share

    def near_peer(step):
        other = (mine + step) % near
        return other, (other // INNER, outer * INNER + other % INNER)

    def far_peer(step):
        other = (outer + step) % far
        return other, (dp, other * INNER + inner)

    def send(source, target, sems, device):
        copy = pltpu.make_async_remote_copy(
            src_ref=source, dst_ref=target, send_sem=sems[0], recv_sem=sems[1],
            device_id=device, device_id_type=pl.DeviceIdType.MESH,
        )
        copy.start()
        return copy

    after, before = (dp, (ctx + 1) % length), (dp, (ctx + length - 1) % length)
    peers = [near_peer(step)[1] for step in range(1, near)]
    peers += [far_peer(step)[1] for step in range(1, far)] + [after, before]
    barrier = pltpu.get_barrier_semaphore()
    for peer in peers:
        pl.semaphore_signal(barrier, inc=1, device_id=peer, device_id_type=pl.DeviceIdType.MESH)
    pl.semaphore_wait(barrier, len(peers))

    copies = []
    for step in range(1, near):
        other, device = near_peer(step)
        copies.append(send(
            sums_ref.at[pl.ds(other * wide, wide)], got_near.at[step - 1],
            (near_send.at[step - 1], near_recv.at[step - 1]), device,
        ))
    edge_copy = send(head_ref, ahead, (edge_sems.at[0], edge_sems.at[1]), before)
    total = sums_ref[pl.ds(mine * wide, wide)]
    for step, copy in enumerate(copies):
        copy.wait()
        total = total + got_near[step]
    part[...] = total

    copies = []
    for step in range(1, far):
        other, device = far_peer(step)
        copies.append(send(
            part.at[pl.ds(other * share, share)], got_far.at[step - 1],
            (far_send.at[step - 1], far_recv.at[step - 1]), device,
        ))
    total = part[pl.ds(outer * share, share)]
    for step, copy in enumerate(copies):
        copy.wait()
        total = total + got_far[step]
    place = pl.ds(mine * wide + outer * share, share)
    full[place] = total * scale

    copies = [
        send(
            full.at[place], full.at[place],
            (far_send2.at[step - 1], far_recv2.at[step - 1]), far_peer(step)[1],
        )
        for step in range(1, far)
    ]
    for copy in copies:
        copy.wait()
    place = pl.ds(mine * wide, wide)
    copies = [
        send(
            full.at[place], full.at[place],
            (near_send2.at[step - 1], near_recv2.at[step - 1]), near_peer(step)[1],
        )
        for step in range(1, near)
    ]
    for copy in copies:
        copy.wait()
    edge_copy.wait()
    out_ref[...] = full[...]
    ahead_ref[...] = ahead[...]


def total_over_devices(sums, head, share, scale):
    f32 = jnp.float32
    span = (lax.axis_size("dp"), lax.axis_size("ctx"))
    near, far = span[0] * INNER, span[1] // INNER
    rows = sums.shape[0]
    vmem = pl.BlockSpec(memory_space=pltpu.VMEM)
    dma = pltpu.SemaphoreType.DMA
    totals, ahead = pl.pallas_call(
        functools.partial(sum_kernel, share, scale, span),
        out_shape=(
            jax.ShapeDtypeStruct((rows, 1, LANES), f32),
            jax.ShapeDtypeStruct(head.shape, head.dtype),
        ),
        in_specs=[vmem] * 2,
        out_specs=(vmem,) * 2,
        scratch_shapes=[
            pltpu.VMEM((near - 1, far * share, 1, LANES), f32),
            pltpu.VMEM((max(far - 1, 1), share, 1, LANES), f32),
            pltpu.VMEM((far * share, 1, LANES), f32),
            pltpu.VMEM((rows, 1, LANES), f32),
            pltpu.VMEM(head.shape, head.dtype),
            dma((near - 1,)), dma((near - 1,)),
            dma((max(far - 1, 1),)), dma((max(far - 1, 1),)),
            dma((max(far - 1, 1),)), dma((max(far - 1, 1),)),
            dma((near - 1,)), dma((near - 1,)),
            dma((2,)),
        ],
        compiler_params=pltpu.CompilerParams(
            collective_id=0, has_side_effects=True, vmem_limit_bytes=16 * 1024 * 1024
        ),
    )(sums.reshape(rows, 1, LANES), head)
    return totals.reshape(rows, LANES), ahead


def body(features, short_w, long_h, skip_bias, cotangent):
    f32, bf16 = jnp.float32, jnp.bfloat16
    feat = features[0]
    cot = cotangent[0]
    rows = feat.shape[0]
    channels = skip_bias.shape[0]
    groups, taps = long_h.shape
    devices = lax.axis_size("dp") * lax.axis_size("ctx")
    used = groups + 10 * (channels // LANES)
    share = -(-used // devices)
    output, grad_in, head, last, sums = main_work(
        feat, cot, short_w, long_h, skip_bias[None], share * devices
    )
    scale = (devices * rows) ** (-0.5)
    totals, ahead = total_over_devices(sums, head, share, scale)
    ahead = jnp.where(lax.axis_index("ctx") + 1 < lax.axis_size("ctx"), ahead, 0.0)
    row0 = last[6] + short_w[2] * ahead[0]
    row1 = last[7] + short_w[1] * ahead[0] + short_w[2] * ahead[1]
    grad_in = lax.dynamic_update_slice(
        grad_in, jnp.stack([row0, row1]).astype(bf16), (rows - 2, 0)
    )
    parts = channels // LANES
    return (
        output[None],
        grad_in[None],
        totals[groups + parts : used].reshape(short_w.shape),
        totals[:groups],
        totals[groups : groups + parts].reshape(channels),
    )


def solution(mesh):
    return jax.shard_map(
        body,
        mesh=mesh,
        in_specs=(P("dp", "ctx", None), P(), P(), P(), P("dp", "ctx", None)),
        out_specs=(P("dp", "ctx", None), P("dp", "ctx", None), P(), P(), P()),
        check_vma=False,
    )
```

time: 88.5 us -> 84.7 us (0.957)
  Pallas kernels: 80.4 us -> 71.8 us
  local copies, waits for them, and re-layouts: 5.34 us -> 9.98 us
    pallas_call x2 -> x1, Pallas kernels: 62.1 us -> 53.3 us  [main_work(): pl.pallas_call(functools.partial(main_kernel, span), out_shape=(jax.Shape...]
    unnamed x6 -> x8, local copies, waits for them, and re-layouts: 1.71 us -> 7.89 us
    slice x1 -> x0, local copies, waits for them, and re-layouts: 1.53 us -> none  [exchange(): feat[rows - 2:]]
where the time goes in v2:
time: 84.7 us; the launch traced here: 84.4 us
  Pallas kernels  71.8 us (85%)
  local copies, waits for them, and re-layouts  9.98 us (12%)
  other arithmetic  1.85 us (2%)
    pallas_call x1, Pallas kernels, main_work(): pl.pallas_call(functools.partial(main_kernel, span), out_shape=(jax.Shape...  53.3 us
    pallas_call x1, Pallas kernels, total_over_devices(): pl.pallas_call(functools.partial(sum_kernel, share, scale, span), out_sha...  18.5 us
    unnamed x8, local copies, waits for them, and re-layouts  7.89 us

profile of v2, /device:TPU:0, one launch (start us, length us, event | category | flops | bytes accessed | tf_op | source)
XLA Modules:
  0.0 84.4 jit_solution(9209067267391334779)
XLA Ops:
  0.6 0.0 copy-start.2
  0.6 53.3 %shard_map.92 = (bf16[256,2048]{1,0:T(8,128)(2,1)}, bf16[256,6144]{1,0:T(8,128)(2,1)}, f32[2,6144]{1,0:T(2,128)}, f32[8,6144]{1,0:T(8,128)}, f32[288,128]{1,0:T(8,128)}) custom-call(bf16[256,6144]{1,0:T(8,128)(2,1)} %bitcast.14, bf16[256,2048]{1,0:T(8,128)(2,1)} %bitcast.16, f32[3,6144]{1,0:T(4,128)} %w_ref.1, f32[128,128]{1,0:T(8,128)} %h_ref.1, ...), custom_call_target="tpu_custom_call" | custom-call | tf_op jit(solution)/shard_map/pallas_call | solution.py:270
  54.0 0.0 copy-start
  54.0 0.9 %copy-done = f32[288,128]{1,0:T(8,128)S(1)} copy-done((f32[288,128]{1,0:T(8,128)S(1)}, f32[288,128]{1,0:T(8,128)}, u32[]{:S(2)}) %copy-start) | copy-done | bytes 147480
  54.9 0.0 copy-start.1
  54.9 0.8 copy-done.1
  55.7 18.5 %shard_map.93 = (f32[288,1,128]{2,1,0:T(1,128)S(1)}, f32[2,6144]{1,0:T(2,128)S(1)}) custom-call(f32[288,1,128]{2,1,0:T(1,128)S(1)} %bitcast.12, f32[2,6144]{1,0:T(2,128)S(1)} %copy-done.1), custom_call_target="tpu_custom_call" | custom-call | tf_op jit(solution)/shard_map/pallas_call | solution.py:400
  74.3 0.0 copy-done.2
  74.3 1.1 %convert_bitcast_fusion.1 = (bf16[1,1,6144]{2,1,0:T(2,128)(2,1)S(1)}, bf16[1,1,6144]{2,1,0:T(2,128)(2,1)S(1)}) fusion(f32[8,6144]{1,0:T(8,128)} %get-tuple-element.14, f32[2,6144]{1,0:T(2,128)S(1)} %broadcast_select_fusion, f32[3,6144]{1,0:T(4,128)S(1)} %copy-done.2), kind=kLoop, calls=%fused_computation.6 | loop fusion | flops 49152 | bytes 172032 | tf_op jit(solution)/shard_map/stack | solution.py:446
  75.4 0.7 maximum_dynamic-update-slice_fusion
  76.1 0.6 slice.43
  76.7 0.6 slice.41
  77.3 0.2 slice_reduce_fusion
  77.5 0.7 reshape.59
  78.2 2.3 %copy.13 = bf16[1,256,2048]{2,1,0:T(8,128)(2,1)} copy(bf16[1,256,2048]{2,1,0:T(8,128)(2,1)} %bitcast.15) | data formatting | bytes 2097152
  80.5 3.9 %copy.14 = bf16[1,256,6144]{2,1,0:T(8,128)(2,1)} copy(bf16[1,256,6144]{2,1,0:T(8,128)(2,1)} %maximum_dynamic-update-slice_fusion) | data formatting | bytes 6291456
  (1 shorter events, 0.0 us)
Async XLA Ops:
  0.6 73.6 %copy-start.2 = (f32[3,6144]{1,0:T(4,128)S(1)}, f32[3,6144]{1,0:T(4,128)}, u32[]{:S(2)}) copy-start(f32[3,6144]{1,0:T(4,128)} %w_ref.1) | copy-start | bytes 221188
  54.0 0.9 %copy-start = (f32[288,128]{1,0:T(8,128)S(1)}, f32[288,128]{1,0:T(8,128)}, u32[]{:S(2)}) copy-start(f32[288,128]{1,0:T(8,128)} %get-tuple-element.15) | copy-start | bytes 442372
  54.9 0.8 copy-start.1

commit v3 on v2

v3 whole, which is shorter than its diff:
```python
import functools

import jax
import jax.numpy as jnp
from jax import lax
from jax.experimental import pallas as pl
from jax.experimental.pallas import tpu as pltpu
from jax.sharding import PartitionSpec as P

LANES = 128
PITCH = 132
INNER = 4
VMEM_LIMIT = 48 * 1024 * 1024


def delayed(tile, edge, by):
    row = lax.broadcasted_iota(jnp.int32, tile.shape, 0)
    moved = pltpu.roll(tile, by, 0)
    if by == 1:
        return jnp.where(row == 0, edge[1:2], moved)
    return jnp.where(row == 0, edge[0:1], jnp.where(row == 1, edge[1:2], moved))


def filtered(feat_ref, w_ref, cols, edge, first, count):
    w = w_ref[:, cols]
    tile = feat_ref[first : first + count, cols].astype(jnp.float32)
    return w[0:1] * tile + w[1:2] * delayed(tile, edge, 1) + w[2:3] * delayed(tile, edge, 2)


def turned_tile(i):
    return pl.ds(i * PITCH, LANES)


def turned_rows(channels):
    return channels // LANES * PITCH


def column_tile(stream, i, channels):
    return pl.ds(pl.multiple_of(stream * channels + i * LANES, LANES), LANES)


def diagonals(kept):
    total = kept[:8]
    for low in range(8, LANES, 8):
        total = total + pltpu.roll(kept[low : low + 8], LANES - low, 1)
    return total


def main_kernel(
    span, scale, feat_hbm, cot_hbm, w_ref, h_ref, skip_ref,
    out_ref, gin_ref, short_ref, long_ref, skip_grad_ref,
    feat_ref, cot_ref, staged, made, grads, zt, gt, rims, mt, gzt, extra, t1_all, lags, lags_rim,
    z_send, g_send, z_rim, g_rim, edge_send, edge_got, edge_ref, head, ahead,
    sums_ref, got_near, part, got_far, full,
    sems, load_sems, near_send, near_recv, far_send, far_recv, near_send2, near_recv2,
):
    rows, channels = cot_ref.shape
    parts = channels // LANES
    groups = h_ref.shape[0]
    blocks = rows // LANES
    f32, bf16 = jnp.float32, jnp.bfloat16
    dps, length = span
    dp, ctx = lax.axis_index("dp"), lax.axis_index("ctx")
    after, before = (dp, (ctx + 1) % length), (dp, (ctx + length - 1) % length)
    near, far = dps * INNER, length // INNER
    outer, inner = ctx // INNER, ctx % INNER
    mine = dp * INNER + inner
    wide = sums_ref.shape[0] // near

    def near_peer(step):
        other = (mine + step) % near
        return other, (other // INNER, outer * INNER + other % INNER)

    def far_peer(step):
        return dp, ((outer + step) % far) * INNER + inner

    has_before = jnp.where(ctx > 0, 1.0, 0.0).astype(f32)
    has_after = jnp.where(ctx + 1 < length, 1.0, 0.0).astype(f32)

    early = rows - LANES - 16
    loads = []
    for source, target in (
        (feat_hbm.at[early:, channels:], feat_ref.at[early:, channels:]),
        (feat_hbm.at[:, :channels], feat_ref.at[:, :channels]),
        (cot_hbm, cot_ref),
        (feat_hbm.at[:early, channels:], feat_ref.at[:early, channels:]),
    ):
        copy = pltpu.make_async_copy(source, target, load_sems.at[len(loads)])
        copy.start()
        loads.append(copy)

    def transfer(source, target, send_sem, recv_sem, device):
        copy = pltpu.make_async_remote_copy(
            src_ref=source, dst_ref=target, send_sem=send_sem, recv_sem=recv_sem,
            device_id=device, device_id_type=pl.DeviceIdType.MESH,
        )
        copy.start()
        return copy

    def send(source, target, index, device):
        return transfer(source, target, sems.at[index], sems.at[index + 1], device)

    peers = [near_peer(step)[1] for step in range(1, near)]
    peers += [far_peer(step) for step in range(1, far)] + [after, before]
    barrier = pltpu.get_barrier_semaphore()
    for peer in peers:
        pl.semaphore_signal(barrier, inc=1, device_id=peer, device_id_type=pl.DeviceIdType.MESH)

    loads[0].wait()
    loads[1].wait()
    edge_send[...] = feat_ref[rows - 16 :, :].astype(f32)[14:16].astype(bf16)
    pl.semaphore_wait(barrier, len(peers))
    edge_copy = send(edge_send, edge_got, 0, after)

    def z_tail(i, _):
        pair = []
        for stream in (1, 2):
            cols = column_tile(stream, i, channels)
            edge = feat_ref[early : early + 16, cols].astype(f32)[14:16]
            pair.append(filtered(feat_ref, w_ref, cols, edge, rows - LANES, LANES))
        z_send[i] = (pair[0] * pair[1]).astype(bf16)
        return 0

    half = parts // 2
    copies = []
    for n in range(2):
        piece = pl.ds(n * half, half)
        lax.fori_loop(n * half, (n + 1) * half, z_tail, 0)
        copies.append(send(z_send.at[piece], z_rim.at[piece], 2 + 2 * n, after))
    edge_copy.wait()
    edge_ref[...] = edge_got[...].astype(f32) * has_before
    loads[2].wait()

    def g_head(i, _):
        own = column_tile(0, i, channels)
        queries = filtered(feat_ref, w_ref, own, edge_ref[:, own], 0, LANES)
        g_send[i] = (cot_ref[:LANES, own].astype(f32) * queries).astype(bf16)
        return 0

    for n in range(2):
        piece = pl.ds(n * half, half)
        lax.fori_loop(n * half, (n + 1) * half, g_head, 0)
        copies.append(send(g_send.at[piece], g_rim.at[piece], 6 + 2 * n, before))
    loads[3].wait()

    def featurize(i, _):
        own = column_tile(0, i, channels)
        for stream in range(3):
            cols = column_tile(stream, i, channels)
            slot = stream * parts + i
            w = w_ref[:, cols]
            staged[slot, 6:8] = edge_ref[:, cols]
            staged[slot, 8:] = feat_ref[:, cols].astype(f32)
            made[slot] = (
                w[0:1] * staged[slot, 8 : 8 + rows]
                + w[1:2] * staged[slot, 7 : 7 + rows]
                + w[2:3] * staged[slot, 6 : 6 + rows]
            )
        total = jnp.zeros((1, LANES), f32)
        for n in range(blocks):
            at = pl.ds(n * LANES, LANES)
            z = (made[parts + i, at] * made[2 * parts + i, at]).astype(bf16).astype(f32)
            g = (cot_ref[at, own].astype(f32) * made[i, at]).astype(bf16).astype(f32)
            total = total + jnp.sum(z * g, axis=0, keepdims=True)
            zt[n, turned_tile(i)] = z.T
            gt[n, turned_tile(i)] = g.T
        sums_ref[pl.ds(groups + i, 1), :] = total
        return 0

    lax.fori_loop(0, parts, featurize, 0)

    s_index = lax.broadcasted_iota(jnp.int32, (LANES, LANES), 0)
    t_index = lax.broadcasted_iota(jnp.int32, (LANES, LANES), 1)
    causal = t_index >= s_index
    contract = lambda a, b, da, db: lax.dot_general(
        a, b, (((da,), (db,)), ((), ())), preferred_element_type=f32
    )

    def convolve(g, _):
        picked = pl.ds(g, parts, stride=PITCH)
        zs = [zt[n, picked].astype(bf16) for n in range(blocks)]
        gs = [gt[n, picked].astype(bf16) for n in range(blocks)]
        none = jnp.zeros((parts, LANES), bf16)
        z_win = jnp.concatenate(
            [jnp.concatenate([a, b], axis=1) for a, b in zip([none] + zs, zs)], axis=0
        )
        g_win = jnp.concatenate(
            [jnp.concatenate([a, b], axis=1) for a, b in zip(gs, gs[1:] + [none])], axis=0
        )
        taps = jnp.broadcast_to(h_ref[pl.ds(g, 1), :].astype(bf16).astype(f32), (LANES, LANES))
        circ = pltpu.roll(taps, 0, 1, stride=1, stride_axis=0)
        t0 = jnp.where(causal, circ, 0.0).astype(bf16)
        t1 = jnp.where(causal, 0.0, circ).astype(bf16)
        t1_all[pl.ds(pl.multiple_of(g * LANES, LANES), LANES)] = t1
        mixed = contract(z_win, jnp.concatenate([t1, t0], axis=0), 1, 0)
        back = contract(g_win, jnp.concatenate([t0, t1], axis=1), 1, 1)
        for n in range(blocks):
            mt[n, picked] = mixed[n * parts : (n + 1) * parts]
            gzt[n, picked] = back[n * parts : (n + 1) * parts]
        prod = contract(z_win, jnp.concatenate(gs, axis=0), 0, 0)
        kept = jnp.where(causal, prod[LANES:], prod[:LANES])
        lags[pl.ds(g, 8, stride=PITCH)] = diagonals(kept)
        return 0

    lax.fori_loop(0, groups, convolve, 0, unroll=8)

    def short_sums(i, stream, n, grad, fresh):
        slot = stream * parts + i
        for tap in range(3):
            low = 8 - tap + n * LANES
            line = pl.ds(groups + parts + (tap * 3 + stream) * parts + i, 1)
            total = jnp.sum(grad * staged[slot, low : low + LANES], axis=0, keepdims=True)
            sums_ref[line, :] = total if fresh else sums_ref[line, :] + total

    def query_part(i, n, fresh, rim):
        own = column_tile(0, i, channels)
        at = pl.ds(n * LANES, LANES)
        q, k, v = made[i, at], made[parts + i, at], made[2 * parts + i, at]
        z = (k * v).astype(bf16).astype(f32)
        mixed = mt[n, turned_tile(i)]
        if rim:
            mixed = mixed + extra[0, turned_tile(i)]
        mixed = mixed.T + skip_ref[:, own] * z
        out_ref[at, own] = (q * mixed).astype(bf16)
        grad = (cot_ref[at, own].astype(f32) * mixed).astype(bf16).astype(f32)
        grads[i, at] = grad
        short_sums(i, 0, n, grad, fresh)

    def pair_part(i, n, fresh, rim):
        own = column_tile(0, i, channels)
        at = pl.ds(n * LANES, LANES)
        q, k, v = made[i, at], made[parts + i, at], made[2 * parts + i, at]
        g = (cot_ref[at, own].astype(f32) * q).astype(bf16).astype(f32)
        grad_z = gzt[n, turned_tile(i)]
        if rim:
            grad_z = grad_z + extra[1, turned_tile(i)]
        grad_z = grad_z.T + skip_ref[:, own] * g
        for stream, other in ((1, v), (2, k)):
            grad = (grad_z * other).astype(bf16).astype(f32)
            grads[stream * parts + i, at] = grad
            short_sums(i, stream, n, grad, fresh)

    def inside(i, _):
        for n in range(1, blocks):
            query_part(i, n, n == 1, False)
        for n in range(blocks - 1):
            pair_part(i, n, n == 0, False)
        return 0

    lax.fori_loop(0, parts, inside, 0)
    for copy in copies:
        copy.wait()

    def turn_rims(i, _):
        rims[0, turned_tile(i)] = (z_rim[i].astype(f32) * has_before).T
        rims[1, turned_tile(i)] = (g_rim[i].astype(f32) * has_after).T
        return 0

    lax.fori_loop(0, parts, turn_rims, 0, unroll=2)

    def convolve_rims(g, _):
        picked = pl.ds(g, parts, stride=PITCH)
        zr = rims[0, picked].astype(bf16)
        gr = rims[1, picked].astype(bf16)
        t1 = t1_all[pl.ds(pl.multiple_of(g * LANES, LANES), LANES)]
        extra[0, picked] = contract(zr, t1, 1, 0)
        extra[1, picked] = contract(gr, t1, 1, 1)
        prod = contract(zr, gt[0, picked].astype(bf16), 0, 0)
        lags_rim[pl.ds(g, 8, stride=PITCH)] = diagonals(jnp.where(causal, 0.0, prod))
        return 0

    lax.fori_loop(0, groups, convolve_rims, 0, unroll=8)
    total = jnp.zeros((groups, LANES), f32)
    for low in range(8):
        at = pl.ds(low * PITCH, groups)
        both = lags[at] + lags_rim[at]
        total = total + (pltpu.roll(both, LANES - low, 1) if low else both)
    sums_ref[:groups] = total

    def rim_part(i, _):
        query_part(i, 0, blocks == 1, True)
        pair_part(i, blocks - 1, blocks == 1, True)
        for stream in range(3):
            head[:, column_tile(stream, i, channels)] = grads[stream * parts + i, 0:2]
        return 0

    lax.fori_loop(0, parts, rim_part, 0)
    used = groups + 10 * parts
    if used < sums_ref.shape[0]:
        sums_ref[used:] = jnp.zeros((sums_ref.shape[0] - used, LANES), f32)

    def share_of(index):
        return pl.ds(pl.multiple_of(index * wide, 8), wide)

    copies = []
    for step in range(1, near):
        other, device = near_peer(step)
        copies.append(transfer(
            sums_ref.at[share_of(other)], got_near.at[step - 1],
            near_send.at[step - 1], near_recv.at[step - 1], device,
        ))
    edge_copy = send(head, ahead, 10, before)

    def adjoint(first, count):
        def one(slot, _):
            cols = pl.ds(pl.multiple_of(slot * LANES, LANES), LANES)
            w = w_ref[:, cols]
            for n in range(first, first + count):
                low = n * LANES
                new = (
                    w[0:1] * grads[slot, low : low + LANES]
                    + w[1:2] * grads[slot, low + 1 : low + 1 + LANES]
                    + w[2:3] * grads[slot, low + 2 : low + 2 + LANES]
                )
                gin_ref[low : low + LANES, cols] = new.astype(bf16)
            return 0

        lax.fori_loop(0, 3 * parts, one, 0)

    adjoint(0, blocks - 1)
    total = sums_ref[share_of(mine)]
    for step, copy in enumerate(copies):
        copy.wait()
        total = total + got_near[step]
    part[...] = total
    copies = [
        transfer(
            part, got_far.at[outer], far_send.at[step - 1], far_recv.at[step - 1], far_peer(step)
        )
        for step in range(1, far)
    ]
    edge_copy.wait()

    def end_rows(slot, _):
        cols = pl.ds(pl.multiple_of(slot * LANES, LANES), LANES)
        grads[slot, rows : rows + 2] = ahead[:, cols] * has_after
        return 0

    lax.fori_loop(0, 3 * parts, end_rows, 0)
    adjoint(blocks - 1, 1)
    got_far[outer] = part[...]
    for copy in copies:
        copy.wait()
    total = got_far[0]
    for step in range(1, far):
        total = total + got_far[step]
    full[share_of(mine)] = total * scale
    copies = [
        transfer(
            full.at[share_of(mine)], full.at[share_of(mine)],
            near_send2.at[step - 1], near_recv2.at[step - 1], near_peer(step)[1],
        )
        for step in range(1, near)
    ]
    for copy in copies:
        copy.wait()
    long_ref[...] = full[:groups]
    for i in range(parts):
        skip_grad_ref[:, i * LANES : (i + 1) * LANES] = full[groups + i : groups + i + 1]
    for tap in range(3):
        for slot in range(3 * parts):
            line = groups + parts + tap * 3 * parts + slot
            short_ref[tap : tap + 1, slot * LANES : (slot + 1) * LANES] = full[line : line + 1]


def body(features, short_w, long_h, skip_bias, cotangent):
    f32, bf16 = jnp.float32, jnp.bfloat16
    feat, cot = features[0], cotangent[0]
    rows, wide = feat.shape
    channels = skip_bias.shape[0]
    parts = channels // LANES
    blocks = rows // LANES
    groups = long_h.shape[0]
    span = (lax.axis_size("dp"), lax.axis_size("ctx"))
    near, far = span[0] * INNER, span[1] // INNER
    used = groups + 10 * parts
    share = -(-used // (8 * near)) * 8
    scale = (span[0] * span[1] * rows) ** (-0.5)
    vmem = pl.BlockSpec(memory_space=pltpu.VMEM)
    hbm = pl.BlockSpec(memory_space=pl.ANY)
    dma = pltpu.SemaphoreType.DMA
    rim = pltpu.VMEM((parts, LANES, LANES), bf16)
    turned = pltpu.VMEM((blocks, turned_rows(channels), LANES), f32)
    turned_pair = pltpu.VMEM((2, turned_rows(channels), LANES), f32)
    output, grad_in, grad_short, grad_long, grad_skip = pl.pallas_call(
        functools.partial(main_kernel, span, scale),
        out_shape=(
            jax.ShapeDtypeStruct((rows, channels), bf16),
            jax.ShapeDtypeStruct((rows, wide), bf16),
            jax.ShapeDtypeStruct((3, wide), f32),
            jax.ShapeDtypeStruct((groups, LANES), f32),
            jax.ShapeDtypeStruct((1, channels), f32),
        ),
        in_specs=[hbm, hbm, vmem, vmem, vmem],
        out_specs=(vmem,) * 5,
        scratch_shapes=[
            pltpu.VMEM((rows, wide), bf16),
            pltpu.VMEM((rows, channels), bf16),
            pltpu.VMEM((3 * parts, rows + 8, LANES), f32),
            pltpu.VMEM((3 * parts, rows, LANES), f32),
            pltpu.VMEM((3 * parts, rows + 8, LANES), f32),
            turned, turned, turned_pair, turned, turned, turned_pair,
            pltpu.VMEM((groups * LANES, LANES), bf16),
            pltpu.VMEM((8 * PITCH, LANES), f32), pltpu.VMEM((8 * PITCH, LANES), f32),
            rim, rim, rim, rim,
            pltpu.VMEM((2, wide), bf16), pltpu.VMEM((2, wide), bf16), pltpu.VMEM((2, wide), f32),
            pltpu.VMEM((2, wide), f32), pltpu.VMEM((2, wide), f32),
            pltpu.VMEM((near * share, LANES), f32),
            pltpu.VMEM((near - 1, share, LANES), f32),
            pltpu.VMEM((share, LANES), f32),
            pltpu.VMEM((far, share, LANES), f32),
            pltpu.VMEM((near * share, LANES), f32),
            dma((12,)), dma((4,)),
            dma((near - 1,)), dma((near - 1,)),
            dma((max(far - 1, 1),)), dma((max(far - 1, 1),)),
            dma((near - 1,)), dma((near - 1,)),
        ],
        compiler_params=pltpu.CompilerParams(
            collective_id=1, has_side_effects=True, vmem_limit_bytes=VMEM_LIMIT
        ),
    )(feat, cot, short_w, long_h, skip_bias[None])
    return output[None], grad_in[None], grad_short, grad_long, grad_skip.reshape(channels)


def solution(mesh):
    return jax.shard_map(
        body,
        mesh=mesh,
        in_specs=(P("dp", "ctx", None), P(), P(), P(), P("dp", "ctx", None)),
        out_specs=(P("dp", "ctx", None), P("dp", "ctx", None), P(), P(), P()),
        check_vma=False,
    )
```

time: 84.7 us -> 64 us (0.76)
  Pallas kernels: 71.8 us -> 54.9 us
  other arithmetic: 1.85 us -> 0 us
  local copies, waits for them, and re-layouts: 9.98 us -> 8.15 us
    pallas_call x2 -> x1, Pallas kernels: 71.8 us -> 54.9 us  [body(): pl.pallas_call(functools.partial(main_kernel, span, scale), out_shape=(ja...]
    slice x3 -> x0, local copies, waits for them, and re-layouts: 1.42 us -> none  [the longest x1 0.63 us: body(): totals[:groups]]
    another operation x1 -> x0, other arithmetic: 1.14 us -> none  [body(): jnp.stack([row0, row1]).astype(bf16)]
    unnamed x8 -> x13, local copies, waits for them, and re-layouts: 7.89 us -> 8.15 us
where the time goes in v3:
time: 64 us; the launch traced here: 63.7 us
  Pallas kernels  54.9 us (86%)
  local copies, waits for them, and re-layouts  8.15 us (13%)
  between operations  0.65 us (1%)
    pallas_call x1, Pallas kernels, body(): pl.pallas_call(functools.partial(main_kernel, span, scale), out_shape=(ja...  54.9 us
    unnamed x13, local copies, waits for them, and re-layouts  8.15 us

profile of v3, /device:TPU:0, one launch (start us, length us, event | category | flops | bytes accessed | tf_op | source)
XLA Modules:
  0.0 63.7 jit_solution(14003636150039720708)
XLA Ops:
  0.6 0.0 copy-start
  0.6 1.2 %copy-done = bf16[1,256,2048]{2,1,0:T(8,128)(2,1)S(1)} copy-done((bf16[1,256,2048]{2,1,0:T(8,128)(2,1)S(1)}, bf16[1,256,2048]{2,1,0:T(8,128)(2,1)}, u32[]{:S(2)}) %copy-start) | copy-done | bytes 1048600
  1.9 0.0 copy-start.1
  1.9 0.9 %copy-done.1 = f32[3,6144]{1,0:T(4,128)S(1)} copy-done((f32[3,6144]{1,0:T(4,128)S(1)}, f32[3,6144]{1,0:T(4,128)}, u32[]{:S(2)}) %copy-start.1) | copy-done | bytes 73752
  2.8 0.0 copy-start.2
  2.8 0.8 %copy-done.2 = f32[128,128]{1,0:T(8,128)S(1)} copy-done((f32[128,128]{1,0:T(8,128)S(1)}, f32[128,128]{1,0:T(8,128)}, u32[]{:S(2)}) %copy-start.2) | copy-done | bytes 65560
  3.6 0.0 copy-start.3
  3.6 0.7 %copy-done.3 = f32[2048]{0:T(1024)S(1)} copy-done((f32[2048]{0:T(1024)S(1)}, f32[2048]{0:T(1024)}, u32[]{:S(2)}) %copy-start.3) | copy-done | bytes 8216
  4.3 54.9 %shard_map.92 = (bf16[256,2048]{1,0:T(8,128)(2,1)S(1)}, bf16[256,6144]{1,0:T(8,128)(2,1)S(1)}, f32[3,6144]{1,0:T(4,128)S(1)}, f32[128,128]{1,0:T(8,128)S(1)}, f32[1,2048]{1,0:T(1,128)S(1)}) custom-call(bf16[256,6144]{1,0:T(8,128)(2,1)} %bitcast.11, bf16[256,2048]{1,0:T(8,128)(2,1)S(1)} %bitcast.8, f32[3,6144]{1,0:T(4,128)S(1)} %copy-done.1, ...), custom_call_target="tpu_custom_call" | custom-call | tf_op jit(solution)/shard_map/pallas_call | solution.py:385
  59.2 1.0 %copy.15 = bf16[1,256,2048]{2,1,0:T(8,128)(2,1)} copy(bf16[1,256,2048]{2,1,0:T(8,128)(2,1)S(1)} %bitcast.7) | data formatting | bytes 2097152
  60.2 1.7 %copy.16 = bf16[1,256,6144]{2,1,0:T(8,128)(2,1)} copy(bf16[1,256,6144]{2,1,0:T(8,128)(2,1)S(1)} %bitcast.6) | data formatting | bytes 6291456
  61.9 0.6 %copy.17 = f32[3,6144]{1,0:T(4,128)} copy(f32[3,6144]{1,0:T(4,128)S(1)} %get-tuple-element.22) | data formatting | bytes 147456
  62.5 0.6 copy.18
  63.1 0.6 copy.19
Async XLA Ops:
  0.6 1.2 %copy-start = (bf16[1,256,2048]{2,1,0:T(8,128)(2,1)S(1)}, bf16[1,256,2048]{2,1,0:T(8,128)(2,1)}, u32[]{:S(2)}) copy-start(bf16[1,256,2048]{2,1,0:T(8,128)(2,1)} %param.9) | copy-start | bytes 3145732
  1.9 0.9 %copy-start.1 = (f32[3,6144]{1,0:T(4,128)S(1)}, f32[3,6144]{1,0:T(4,128)}, u32[]{:S(2)}) copy-start(f32[3,6144]{1,0:T(4,128)} %w_ref.1) | copy-start | bytes 221188
  2.8 0.8 %copy-start.2 = (f32[128,128]{1,0:T(8,128)S(1)}, f32[128,128]{1,0:T(8,128)}, u32[]{:S(2)}) copy-start(f32[128,128]{1,0:T(8,128)} %h_ref.1) | copy-start | bytes 196612
  3.6 0.7 %copy-start.3 = (f32[2048]{0:T(1024)S(1)}, f32[2048]{0:T(1024)}, u32[]{:S(2)}) copy-start(f32[2048]{0:T(1024)} %param.8) | copy-start | bytes 24580

commit v4 on v3

--- a/solution.py
+++ b/solution.py
@@ -47,9 +47,9 @@
 
 
 def main_kernel(
-    span, scale, feat_hbm, cot_hbm, w_ref, h_ref, skip_ref,
+    span, scale, feat_hbm, cot_hbm, w_hbm, h_hbm, skip_hbm,
     out_ref, gin_ref, short_ref, long_ref, skip_grad_ref,
-    feat_ref, cot_ref, staged, made, grads, zt, gt, rims, mt, gzt, extra, t1_all, lags, lags_rim,
+    feat_ref, cot_ref, w_ref, h_ref, skip_ref, staged, made, grads, zt, gt, rims, mt, gzt, extra, t1_all, lags, lags_rim,
     z_send, g_send, z_rim, g_rim, edge_send, edge_got, edge_ref, head, ahead,
     sums_ref, got_near, part, got_far, full,
     sems, load_sems, near_send, near_recv, far_send, far_recv, near_send2, near_recv2,
@@ -81,9 +81,12 @@
     loads = []
     for source, target in (
         (feat_hbm.at[early:, channels:], feat_ref.at[early:, channels:]),
+        (w_hbm, w_ref),
         (feat_hbm.at[:, :channels], feat_ref.at[:, :channels]),
         (cot_hbm, cot_ref),
         (feat_hbm.at[:early, channels:], feat_ref.at[:early, channels:]),
+        (h_hbm, h_ref),
+        (skip_hbm, skip_ref),
     ):
         copy = pltpu.make_async_copy(source, target, load_sems.at[len(loads)])
         copy.start()
@@ -106,8 +109,8 @@
     for peer in peers:
         pl.semaphore_signal(barrier, inc=1, device_id=peer, device_id_type=pl.DeviceIdType.MESH)
 
-    loads[0].wait()
-    loads[1].wait()
+    for load in loads[:3]:
+        load.wait()
     edge_send[...] = feat_ref[rows - 16 :, :].astype(f32)[14:16].astype(bf16)
     pl.semaphore_wait(barrier, len(peers))
     edge_copy = send(edge_send, edge_got, 0, after)
@@ -129,7 +132,7 @@
         copies.append(send(z_send.at[piece], z_rim.at[piece], 2 + 2 * n, after))
     edge_copy.wait()
     edge_ref[...] = edge_got[...].astype(f32) * has_before
-    loads[2].wait()
+    loads[3].wait()
 
     def g_head(i, _):
         own = column_tile(0, i, channels)
@@ -141,7 +144,8 @@
         piece = pl.ds(n * half, half)
         lax.fori_loop(n * half, (n + 1) * half, g_head, 0)
         copies.append(send(g_send.at[piece], g_rim.at[piece], 6 + 2 * n, before))
-    loads[3].wait()
+    for load in loads[4:]:
+        load.wait()
 
     def featurize(i, _):
         own = column_tile(0, i, channels)
@@ -269,7 +273,7 @@
         lags_rim[pl.ds(g, 8, stride=PITCH)] = diagonals(jnp.where(causal, 0.0, prod))
         return 0
 
-    lax.fori_loop(0, groups, convolve_rims, 0, unroll=8)
+    lax.fori_loop(0, groups, convolve_rims, 0, unroll=16)
     total = jnp.zeros((groups, LANES), f32)
     for low in range(8):
         at = pl.ds(low * PITCH, groups)
@@ -363,6 +367,15 @@
             short_ref[tap : tap + 1, slot * LANES : (slot + 1) * LANES] = full[line : line + 1]
 
 
+def store_kernel(*refs):
+    sems = refs[10]
+    copies = [pltpu.make_async_copy(refs[n], refs[5 + n], sems.at[n]) for n in range(5)]
+    for copy in copies:
+        copy.start()
+    for copy in copies:
+        copy.wait()
+
+
 def body(features, short_w, long_h, skip_bias, cotangent):
     f32, bf16 = jnp.float32, jnp.bfloat16
     feat, cot = features[0], cotangent[0]
@@ -377,12 +390,12 @@
     share = -(-used // (8 * near)) * 8
     scale = (span[0] * span[1] * rows) ** (-0.5)
     vmem = pl.BlockSpec(memory_space=pltpu.VMEM)
-    hbm = pl.BlockSpec(memory_space=pl.ANY)
+    hbm = pl.BlockSpec(memory_space=pltpu.HBM)
     dma = pltpu.SemaphoreType.DMA
     rim = pltpu.VMEM((parts, LANES, LANES), bf16)
     turned = pltpu.VMEM((blocks, turned_rows(channels), LANES), f32)
     turned_pair = pltpu.VMEM((2, turned_rows(channels), LANES), f32)
-    output, grad_in, grad_short, grad_long, grad_skip = pl.pallas_call(
+    results = pl.pallas_call(
         functools.partial(main_kernel, span, scale),
         out_shape=(
             jax.ShapeDtypeStruct((rows, channels), bf16),
@@ -391,11 +404,14 @@
             jax.ShapeDtypeStruct((groups, LANES), f32),
             jax.ShapeDtypeStruct((1, channels), f32),
         ),
-        in_specs=[hbm, hbm, vmem, vmem, vmem],
+        in_specs=[hbm] * 5,
         out_specs=(vmem,) * 5,
         scratch_shapes=[
             pltpu.VMEM((rows, wide), bf16),
             pltpu.VMEM((rows, channels), bf16),
+            pltpu.VMEM(short_w.shape, f32),
+            pltpu.VMEM(long_h.shape, f32),
+            pltpu.VMEM((1, channels), f32),
             pltpu.VMEM((3 * parts, rows + 8, LANES), f32),
             pltpu.VMEM((3 * parts, rows, LANES), f32),
             pltpu.VMEM((3 * parts, rows + 8, LANES), f32),
@@ -410,7 +426,7 @@
             pltpu.VMEM((share, LANES), f32),
             pltpu.VMEM((far, share, LANES), f32),
             pltpu.VMEM((near * share, LANES), f32),
-            dma((12,)), dma((4,)),
+            dma((12,)), dma((7,)),
             dma((near - 1,)), dma((near - 1,)),
             dma((max(far - 1, 1),)), dma((max(far - 1, 1),)),
             dma((near - 1,)), dma((near - 1,)),
@@ -419,6 +435,14 @@
             collective_id=1, has_side_effects=True, vmem_limit_bytes=VMEM_LIMIT
         ),
     )(feat, cot, short_w, long_h, skip_bias[None])
+    output, grad_in, grad_short, grad_long, grad_skip = pl.pallas_call(
+        store_kernel,
+        out_shape=tuple(jax.ShapeDtypeStruct(r.shape, r.dtype) for r in results),
+        in_specs=[vmem] * 5,
+        out_specs=(hbm,) * 5,
+        scratch_shapes=[dma((5,))],
+        compiler_params=pltpu.CompilerParams(vmem_limit_bytes=1024 * 1024),
+    )(*results)
     return output[None], grad_in[None], grad_short, grad_long, grad_skip.reshape(channels)
 
 

time: 64 us -> 60.1 us (0.939)
  local copies, waits for them, and re-layouts: 8.15 us -> 3.65 us
    unnamed x13 -> x8, local copies, waits for them, and re-layouts: 8.15 us -> 3.65 us
    pallas_call x0 -> x1, Pallas kernels: none -> 2.09 us  [body(): pl.pallas_call(store_kernel, out_shape=tuple((jax.ShapeDtypeStruct(r.shap...]
    pallas_call x1, Pallas kernels: 54.9 us -> 53.4 us  [body(): pl.pallas_call(functools.partial(main_kernel, span, scale), out_shape=(ja...]
where the time goes in v4:
time: 60.1 us; the launch traced here: 59.8 us
  Pallas kernels  55.5 us (92%)
  local copies, waits for them, and re-layouts  3.65 us (6%)
  between operations  0.65 us (1%)
    pallas_call x1, Pallas kernels, body(): pl.pallas_call(functools.partial(main_kernel, span, scale), out_shape=(ja...  53.4 us
    unnamed x8, local copies, waits for them, and re-layouts  3.65 us
    pallas_call x1, Pallas kernels, body(): pl.pallas_call(store_kernel, out_shape=tuple((jax.ShapeDtypeStruct(r.shap...  2.09 us

profile of v4, /device:TPU:0, one launch (start us, length us, event | category | flops | bytes accessed | tf_op | source)
XLA Modules:
  0.0 59.8 jit_solution(16186916797732893535)
XLA Ops:
  0.6 0.0 copy-start
  0.6 1.2 %copy-done = bf16[1,256,2048]{2,1,0:T(8,128)(2,1)S(1)} copy-done((bf16[1,256,2048]{2,1,0:T(8,128)(2,1)S(1)}, bf16[1,256,2048]{2,1,0:T(8,128)(2,1)}, u32[]{:S(2)}) %copy-start) | copy-done | bytes 1048600
  1.9 0.0 copy-start.1
  1.9 0.9 %copy-done.1 = f32[3,6144]{1,0:T(4,128)S(1)} copy-done((f32[3,6144]{1,0:T(4,128)S(1)}, f32[3,6144]{1,0:T(4,128)}, u32[]{:S(2)}) %copy-start.1) | copy-done | bytes 73752
  2.8 0.0 copy-start.2
  2.8 0.8 %copy-done.2 = f32[128,128]{1,0:T(8,128)S(1)} copy-done((f32[128,128]{1,0:T(8,128)S(1)}, f32[128,128]{1,0:T(8,128)}, u32[]{:S(2)}) %copy-start.2) | copy-done | bytes 65560
  3.6 0.0 copy-start.3
  3.6 0.7 %copy-done.3 = f32[2048]{0:T(1024)S(1)} copy-done((f32[2048]{0:T(1024)S(1)}, f32[2048]{0:T(1024)}, u32[]{:S(2)}) %copy-start.3) | copy-done | bytes 8216
  4.3 53.4 %shard_map.92 = (bf16[256,2048]{1,0:T(8,128)(2,1)S(1)}, bf16[256,6144]{1,0:T(8,128)(2,1)S(1)}, f32[3,6144]{1,0:T(4,128)S(1)}, f32[128,128]{1,0:T(8,128)S(1)}, f32[1,2048]{1,0:T(1,128)S(1)}) custom-call(bf16[256,6144]{1,0:T(8,128)(2,1)} %bitcast.8, bf16[256,2048]{1,0:T(8,128)(2,1)S(1)} %bitcast.6, f32[3,6144]{1,0:T(4,128)S(1)} %copy-done.1, ...), custom_call_target="tpu_custom_call" | custom-call | tf_op jit(solution)/shard_map/pallas_call | solution.py:398
  57.7 2.1 %shard_map.93 = (bf16[256,2048]{1,0:T(8,128)(2,1)}, bf16[256,6144]{1,0:T(8,128)(2,1)}, f32[3,6144]{1,0:T(4,128)}, f32[128,128]{1,0:T(8,128)}, f32[1,2048]{1,0:T(1,128)}) custom-call(bf16[256,2048]{1,0:T(8,128)(2,1)S(1)} %get-tuple-element.15.refs_0_, bf16[256,6144]{1,0:T(8,128)(2,1)S(1)} %get-tuple-element.16.refs_1_, ...), custom_call_target="tpu_custom_call" | custom-call | tf_op jit(solution)/shard_map/pallas_call | solution.py:438
Async XLA Ops:
  0.6 1.2 %copy-start = (bf16[1,256,2048]{2,1,0:T(8,128)(2,1)S(1)}, bf16[1,256,2048]{2,1,0:T(8,128)(2,1)}, u32[]{:S(2)}) copy-start(bf16[1,256,2048]{2,1,0:T(8,128)(2,1)} %param.9) | copy-start | bytes 3145732
  1.9 0.9 %copy-start.1 = (f32[3,6144]{1,0:T(4,128)S(1)}, f32[3,6144]{1,0:T(4,128)}, u32[]{:S(2)}) copy-start(f32[3,6144]{1,0:T(4,128)} %w_hbm.1) | copy-start | bytes 221188
  2.8 0.8 %copy-start.2 = (f32[128,128]{1,0:T(8,128)S(1)}, f32[128,128]{1,0:T(8,128)}, u32[]{:S(2)}) copy-start(f32[128,128]{1,0:T(8,128)} %h_hbm.1) | copy-start | bytes 196612
  3.6 0.7 %copy-start.3 = (f32[2048]{0:T(1024)S(1)}, f32[2048]{0:T(1024)}, u32[]{:S(2)}) copy-start(f32[2048]{0:T(1024)} %param.8) | copy-start | bytes 24580
